TPU v7x, 32 devices: a whole 2x2x4 slice. The times are simulated.
32 devices in a mesh: seq: 16 (over z, y, x), head: 2 (over core).
Axes of the slice: x: 2, y: 2, z: 4, core: 2. Of those that a mesh axis runs over, the one named last changes fastest.
Arguments:
- queries: bfloat16 [2048, 16, 128], P('seq', 'head'), may hold values from -6 to 6
- key_vectors: bfloat16 [2048, 16, 128], P('seq', 'head'), may hold values from -16 to 16
- values: bfloat16 [2048, 16, 128], P('seq', 'head'), may hold values from -6 to 6
- out_gate: bfloat16 [2048, 16, 128], P('seq', 'head'), may hold values from -6 to 6
- inputs: bfloat16 [2048, 2048], P('seq', 'head'), may hold values from -6 to 6
- beta_weight: bfloat16 [16, 2048], P(None, 'head'), may hold values from -0.1875 to 0.1875
- log_decay: float32 [16, 2048], P('head', 'seq'), may hold values from -1 to 0
- initial_state: float32 [16, 128, 128], P('head'), may hold values from -6 to 6
Outputs:
- gated_out: bfloat16 [2048, 16, 128], P('seq', 'head')
- block_states: float32 [32, 16, 128, 128], P('seq', 'head')
All inputs are finite; a program needn't handle non-finite values.
Results may differ from a plain program's by a relative error of at most 0.0012.
Values sent between devices are 32-bit elements; how exact they have to be, the bound alone decides.
No kernel may reach another device: no remote copies, remote signals or barrier semaphores. Data moves between devices by JAX's collectives and lax.ppermute only.
A program may use at most 64 MiB of HBM per device.

v0:
```python
import jax
import jax.numpy as jnp
from jax import lax
from jax.sharding import PartitionSpec as P

BLOCK = 64
EPSILON = 1e-06


def entering(value, axis, join, neutral):
    count, mine = (lax.axis_size(axis), lax.axis_index(axis))
    pieces = jax.tree.map(lambda part: lax.all_gather(part, axis), value)
    so_far = jax.tree.map(
        lambda part, zero: jnp.full_like(part, 0) + jnp.asarray(zero, part.dtype), value, neutral
    )

    def step(position, so_far):
        longer = join(so_far, jax.tree.map(lambda part: part[position], pieces))
        return jax.tree.map(lambda new, old: jnp.where(position < mine, new, old), longer, so_far)

    return lax.fori_loop(0, count - 1, step, so_far)


def matmul(matrix, operand):
    return jnp.einsum("...ij,...jk->...ik", matrix, operand, precision=lax.Precision.HIGHEST)


def normalize(query_block, key_block, key_limit):
    query_float = query_block.astype(jnp.float32)
    key_float = key_block.astype(jnp.float32)
    queries_unit = (
        query_float
        / jnp.sqrt(jnp.sum(query_float * query_float, -1, keepdims=True) + EPSILON)
        * query_float.shape[-1] ** (-0.5)
    )
    keys_unit = key_float / jnp.maximum(
        jnp.sqrt(jnp.sum(key_float * key_float, -1, keepdims=True)), key_limit
    )
    return (queries_unit, keys_unit)


def block_parts(queries_unit, keys_unit, value_rows, beta_gate, decay_rows):
    length = decay_rows.shape[-1]
    feature = keys_unit.shape[-1]
    cumulative = jnp.cumsum(decay_rows, axis=-1)
    inside = jnp.tril(jnp.ones((length, length), jnp.float32))
    strict = jnp.tril(jnp.ones((length, length), jnp.float32), -1)
    spread = jnp.where(inside > 0, cumulative[..., :, None] - cumulative[..., None, :], 0.0)
    damping = jnp.exp(spread) * inside
    intersections = jnp.einsum(
        "...id,...jd->...ij", keys_unit, keys_unit, precision=lax.Precision.HIGHEST
    )
    system = (
        jnp.eye(length, dtype=jnp.float32)
        + beta_gate[..., :, None] * intersections * damping * strict
    )
    right_side = jnp.concatenate(
        [
            (beta_gate * jnp.exp(cumulative))[..., None] * keys_unit,
            beta_gate[..., None] * value_rows,
        ],
        axis=-1,
    )
    solved = lax.linalg.triangular_solve(
        system, right_side, left_side=True, lower=True, unit_diagonal=True
    )
    write_keys = solved[..., :feature]
    write_values = solved[..., feature:]
    final_sum = cumulative[..., -1:]
    carried = keys_unit * jnp.exp(final_sum - cumulative)[..., None]
    transition = jnp.exp(final_sum)[..., None] * jnp.eye(feature, dtype=jnp.float32) - jnp.einsum(
        "...ld,...le->...de", carried, write_keys, precision=lax.Precision.HIGHEST
    )
    offset = jnp.einsum(
        "...ld,...le->...de", carried, write_values, precision=lax.Precision.HIGHEST
    )
    reached = queries_unit * jnp.exp(cumulative)[..., None]
    scores = (
        jnp.einsum("...id,...jd->...ij", queries_unit, keys_unit, precision=lax.Precision.HIGHEST)
        * damping
    )
    return (write_keys, write_values, transition, offset, reached, scores)


def block_out(block_info, state_now):
    write_keys, write_values, transition, offset, reached, scores = block_info
    corrected = write_values - matmul(write_keys, state_now)
    return matmul(reached, state_now) + matmul(scores, corrected)


def gate_norm(raw_out, gate_rows):
    inverse_rms = 1.0 / jnp.sqrt(jnp.mean(raw_out * raw_out, -1, keepdims=True) + EPSILON)
    return (raw_out * inverse_rms * jax.nn.silu(gate_rows.astype(jnp.float32))).astype(jnp.bfloat16)


def combine(earlier, latter):
    return (matmul(latter[0], earlier[0]), matmul(latter[0], earlier[1]) + latter[1])


def advance(queries_unit, keys_unit, value_rows, beta_gate, decay_rows, start_state):
    block_info = block_parts(queries_unit, keys_unit, value_rows, beta_gate, decay_rows)
    transition = jnp.moveaxis(block_info[2], 1, 0)
    offset = jnp.moveaxis(block_info[3], 1, 0)
    head_count = transition.shape[1]
    feature = transition.shape[2]
    identity_map = jnp.broadcast_to(
        jnp.eye(feature, dtype=jnp.float32), (head_count, feature, feature)
    )
    zero_state = jnp.zeros((head_count, feature, value_rows.shape[-1]), jnp.float32)

    def compose(carried_map, block_map):
        return (
            (
                matmul(block_map[0], carried_map[0]),
                matmul(block_map[0], carried_map[1]) + block_map[1],
            ),
            carried_map,
        )

    (device_map, device_offset), prefixes = lax.scan(
        compose, (identity_map, zero_state), (transition, offset)
    )
    before_map, before_offset = entering(
        (device_map, device_offset), "seq", combine, (identity_map, zero_state)
    )
    entry_state = matmul(before_map, start_state) + before_offset
    starts = matmul(prefixes[0], entry_state[None]) + prefixes[1]
    raw_out = block_out(block_info, jnp.moveaxis(starts, 0, 1))
    return (raw_out, starts)


def on_device(
    queries, key_vectors, values, out_gate, inputs, beta_weight, log_decay, initial_state
):
    token_count, head_count, feature = queries.shape
    blocks = token_count // BLOCK
    logits = lax.psum_scatter(
        lax.dot_general(
            beta_weight, inputs, (((1,), (1,)), ((), ())), preferred_element_type=jnp.float32
        ),
        "head",
        scatter_dimension=0,
        tiled=True,
    )
    beta_gate = jax.nn.sigmoid(logits)
    key_float = key_vectors.astype(jnp.float32)
    key_total = lax.psum(jnp.sum(key_float * key_float, axis=(0, 2)), "seq")
    key_limit = jnp.sqrt(key_total / (token_count * lax.axis_size("seq")) + EPSILON)
    queries_unit, keys_unit = normalize(queries, key_vectors, key_limit[:, None])

    def arrange(tensor):
        return tensor.reshape(blocks, BLOCK, head_count, -1).transpose(2, 0, 1, 3)

    query_blocks = arrange(queries_unit)
    key_blocks = arrange(keys_unit)
    value_blocks = arrange(values.astype(jnp.float32))
    beta_blocks = beta_gate.reshape(head_count, blocks, BLOCK)
    decay_blocks = log_decay.reshape(head_count, blocks, BLOCK)
    raw_out, starts = advance(
        query_blocks, key_blocks, value_blocks, beta_blocks, decay_blocks, initial_state
    )
    gated_out = gate_norm(
        raw_out.transpose(1, 2, 0, 3).reshape(token_count, head_count, feature), out_gate
    )
    return (gated_out, starts)


def solution(mesh):
    return jax.shard_map(
        on_device,
        mesh=mesh,
        in_specs=(
            P("seq", "head", None),
            P("seq", "head", None),
            P("seq", "head", None),
            P("seq", "head", None),
            P("seq", "head"),
            P(None, "head"),
            P("head", "seq"),
            P("head", None, None),
        ),
        out_specs=(P("seq", "head", None), P("seq", "head", None, None)),
        check_vma=False,
    )
```

profile of v0, /device:TPU:0, one launch (start us, length us, event | category | flops | bytes accessed | tf_op | source)
XLA Modules:
  0.0 458.2 jit_solution(17087418341831936964)
XLA Ops:
  10.1 43.5 %psum.7 = f32[8]{0:T(128)S(1)} all-reduce(f32[8]{0:T(128)S(1)} %get-tuple-element.239), channel_id=1, replica_groups=mesh['seq'=16,'head'=2] {'seq'}, use_global_device_ids=true, to_apply=%region_4.0 | all-reduce | flops 8 | bytes 64 | tf_op jit(solution)/shard_map/psum | solution.py:147
  55.0 1.3 fusion.68
  56.3 2.5 all-reduce
  61.8 78.6 %custom-call.3 = f32[8,2,1,64,64]{3,4,2,1,0:T(8,128)S(1)} custom-call(f32[8,2,1,64,64]{4,3,2,1,0:T(8,128)S(1)} %fusion.30), custom_call_target="InvertDiagBlocksLowerTriangular" | custom-call | tf_op jit(solution)/shard_map/triangular_solve | solution.py:64
  143.0 3.0 convolution_bitcast_fusion
  146.0 2.0 fusion.22
  148.1 12.5 %while.33 = (s32[]{:T(128)}, f32[8,128,128]{2,1,0:T(8,128)S(1)}, f32[8,128,128]{2,1,0:T(8,128)}, f32[2,8,128,128]{3,2,0,1:T(8,128)}, f32[2,8,128,128]{2,3,0,1:T(...) while((s32[]{:T(128)}, f32[8,128,128]{2,1,0:T(8,128)S(1)}, ...), condition=%wide.region_7.8_spmd.clone, body=%wide.region_6.7_spmd.clone.sunk | while | flops 403046400 | bytes 9963628 | solution.py:120
  149.2 2.5 convolution_add_fusion.5
  155.4 2.5 convolution_add_fusion.5
  162.7 2.8 convolution_multiply_fusion
  165.5 104.3 %all-gather.5.cloned.1.call-done = f32[128,128,128]{2,1,0:T(8,128)} async-done(((f32[8,128,128]{2,1,0:T(8,128)}), f32[128,128,128]{2,1,0:T(8,128)}) %all-gather.5.cloned.1.call-update) | async-done | bytes 8388624 | tf_op jit(solution)/shard_map/all_gather | solution.py:12
  269.8 113.3 %all-gather.7.cloned.1.call-done = f32[128,128,128]{2,1,0:T(8,128)} async-done(((f32[8,128,128]{2,1,0:T(8,128)}), f32[128,128,128]{2,1,0:T(8,128)}) %all-gather.7.cloned.1.call-update) | async-done | bytes 8388624 | tf_op jit(solution)/shard_map/all_gather | solution.py:12
  383.1 55.4 %while.34 = (s32[]{:T(128)}, f32[8,128,128]{2,1,0:T(8,128)S(1)}, f32[8,128,128]{2,1,0:T(8,128)S(1)}, s32[]{:T(128)}, f32[16,8,128,128]{3,2,1,0:T(8,128)}, /*index=5*/f32[16,8,128,128]{3,2,1,0:T(8,128)}, s32[]{:T(128)}, s32[]{:T(128)}) while((s32[]{:T(128)}, f32[8,128,128]{2,1,0:T(8,128)S(1)}, f32[8,128,128]{2,1,0:T(8,128)S(1)}, ...), condition=%wide.region_9.10_spmd.clone, body=%wide.region_8.9_spmd.clone.sunk | while | flops 403308544 | bytes 6818920 | solution.py:21
  383.2 1.9 fusion.102
  385.2 1.7 convolution_select_fusion.2
  386.9 1.9 fusion.102
  388.9 1.7 convolution_select_fusion.2
  390.6 1.9 fusion.102
  392.5 1.7 convolution_select_fusion.2
  394.3 1.9 fusion.102
  396.2 1.7 convolution_select_fusion.2
  398.0 1.9 fusion.102
  399.9 1.7 convolution_select_fusion.2
  401.7 1.9 fusion.102
  403.6 1.7 convolution_select_fusion.2
  405.4 1.9 fusion.102
  407.3 1.7 convolution_select_fusion.2
  409.1 1.9 fusion.102
  411.0 1.7 convolution_select_fusion.2
  412.8 1.9 fusion.102
  414.7 1.7 convolution_select_fusion.2
  416.4 1.9 fusion.102
  418.4 1.7 convolution_select_fusion.2
  420.1 1.9 fusion.102
  422.1 1.7 convolution_select_fusion.2
  423.8 1.9 fusion.102
  425.7 1.7 convolution_select_fusion.2
  427.5 1.9 fusion.102
  429.4 1.7 convolution_select_fusion.2
  431.2 1.9 fusion.102
  433.1 1.7 convolution_select_fusion.2
  434.9 1.9 fusion.102
  436.8 1.7 convolution_select_fusion.2
  439.2 2.6 fusion.23
  441.8 2.9 convolution_subtract_fusion
  444.7 1.3 copy.94
  446.0 1.8 fusion.69
  447.9 2.2 fusion.45
  (103 shorter events, 21.5 us)
Async XLA Ops:
  7.2 431.4 %copy-start = (f32[8,128,128]{2,1,0:T(8,128)S(1)}, f32[8,128,128]{2,1,0:T(8,128)}, u32[]{:S(2)}) copy-start(f32[8,128,128]{2,1,0:T(8,128)} %param.19) | copy-start | bytes 1572868
  7.2 262.6 %all-gather.5.cloned.1.call-start = ((), (), s32[]{:S(2)}) async-start(), calls=%async_computation | async-start | bytes 8912896 | tf_op jit(solution)/shard_map/all_gather | solution.py:12
  55.0 91.0 %copy-start.2 = (f32[128,8,128]{2,0,1:T(8,128)}, f32[128,8,128]{2,0,1:T(8,128)S(1)}, u32[]{:S(2)}) copy-start(f32[128,8,128]{2,0,1:T(8,128)S(1)} %copy.77) | copy-start | bytes 1572868
  143.0 5.0 %copy-start.3 = (f32[8,2,64,256]{3,2,1,0:T(8,128)}, f32[8,2,64,256]{3,2,1,0:T(8,128)S(1)}, u32[]{:S(2)}) copy-start(f32[8,2,64,256]{3,2,1,0:T(8,128)S(1)} %fusion.31) | copy-start | bytes 3145732
  148.1 14.1 %copy-start.5 = (bf16[128,8,128]{2,1,0:T(8,128)(2,1)S(1)}, bf16[128,8,128]{2,1,0:T(8,128)(2,1)}, u32[]{:S(2)}) copy-start(bf16[128,8,128]{2,1,0:T(8,128)(2,1)} %param.12) | copy-start | bytes 786436
  160.6 0.8 copy-start.1
  161.4 221.7 %all-gather.7.cloned.1.call-start = ((), (), s32[]{:S(2)}) async-start(), calls=%async_computation.1 | async-start | bytes 8912896 | tf_op jit(solution)/shard_map/all_gather | solution.py:12
  383.1 58.7 %copy-start.4 = (f32[8,2,64,256]{3,2,1,0:T(8,128)S(1)}, f32[8,2,64,256]{3,2,1,0:T(8,128)}, u32[]{:S(2)}) copy-start(f32[8,2,64,256]{3,2,1,0:T(8,128)} %copy-done.3) | copy-start | bytes 3145732
  438.5 11.7 %copy-start.6 = (bf16[128,8,128]{2,1,0:T(8,128)(2,1)S(1)}, bf16[128,8,128]{2,1,0:T(8,128)(2,1)}, u32[]{:S(2)}) copy-start(bf16[128,8,128]{2,1,0:T(8,128)(2,1)} %param.15) | copy-start | bytes 786436
Sparse Core Ops, SparseCore 0:
  161.5 108.2 all-gather.4
  272.6 110.4 all-gather.6
where the time goes:
time: 460 us; the launch traced here: 458 us
  waiting for transfers between devices  218 us (47%)
  other arithmetic  83.8 us (18%)
  matrix products  81.3 us (18%)
  blocking collectives  46 us (10%)
  between operations  15 us (3%)
  local copies, waits for them, and re-layouts  12.8 us (3%)
    all_gather x2, waiting for transfers between devices, entering(): pieces = jax.tree.map(lambda part: lax.all_gather(part, axis), value)  218 us
    another operation x4, other arithmetic, block_parts(): lax.linalg.triangular_solve(system, right_side, left_side=True, lower=Tru...  78.7 us
    dot_general x39, matrix products, matmul(): jnp.einsum('...ij,...jk->...ik', matrix, operand, precision=lax.Precision...  70 us
    psum x1, blocking collectives, on_device(): key_total = lax.psum(jnp.sum(key_float * key_float, axis=(0, 2)), 'seq')  43.5 us
  transfers between devices with their start and end apart: 2, of which 2 were waited for; matrix products, arithmetic and copies ran while one was open for 1% of the time, Pallas kernels for 0%

commit v1 on v0

--- a/solution.py
+++ b/solution.py
@@ -144,7 +144,7 @@
     )
     beta_gate = jax.nn.sigmoid(logits)
     key_float = key_vectors.astype(jnp.float32)
-    key_total = lax.psum(jnp.sum(key_float * key_float, axis=(0, 2)), "seq")
+    key_total = jnp.sum(lax.all_gather(jnp.sum(key_float * key_float, axis=(0, 2)), "seq"), axis=0)
     key_limit = jnp.sqrt(key_total / (token_count * lax.axis_size("seq")) + EPSILON)
     queries_unit, keys_unit = normalize(queries, key_vectors, key_limit[:, None])
 

time: 460 us -> 462 us (level)
    psum x1 -> x0, blocking collectives: 43.5 us -> none  [on_device(): key_total = lax.psum(jnp.sum(key_float * key_float, axis=(0, 2)), 'seq')]
    unnamed x1 -> x2, blocking collectives: 2.49 us -> 46 us
where the time goes in v1:
time: 462 us; the launch traced here: 460 us
  waiting for transfers between devices  218 us (47%)
  other arithmetic  83.8 us (18%)
  matrix products  81.3 us (18%)
  blocking collectives  46 us (10%)
  between operations  15.7 us (3%)
  local copies, waits for them, and re-layouts  14.4 us (3%)
    all_gather x2, waiting for transfers between devices, entering(): pieces = jax.tree.map(lambda part: lax.all_gather(part, axis), value)  218 us
    another operation x4, other arithmetic, block_parts(): lax.linalg.triangular_solve(system, right_side, left_side=True, lower=Tru...  78.7 us
    dot_general x39, matrix products, matmul(): jnp.einsum('...ij,...jk->...ik', matrix, operand, precision=lax.Precision...  70 us
    unnamed x2, blocking collectives  46 us
  transfers between devices with their start and end apart: 2, of which 2 were waited for; matrix products, arithmetic and copies ran while one was open for 1% of the time, Pallas kernels for 0%

profile of v1, /device:TPU:0, one launch (start us, length us, event | category | flops | bytes accessed | tf_op | source)
XLA Modules:
  0.0 460.5 jit_solution(11357983003086680550)
XLA Ops:
  12.3 43.5 %all-reduce = f32[128]{0:T(128)S(1)} all-reduce(f32[128]{0:T(128)S(1)} %dynamic-update-slice), channel_id=2, replica_groups=mesh['seq'=16,'head'=2] {'seq'}, use_global_device_ids=true, to_apply=%add | all-reduce | flops 128 | bytes 1024
  57.2 1.3 fusion.68
  58.6 2.5 all-reduce.1
  64.0 78.6 %custom-call.3 = f32[8,2,1,64,64]{3,4,2,1,0:T(8,128)S(1)} custom-call(f32[8,2,1,64,64]{4,3,2,1,0:T(8,128)S(1)} %fusion.30), custom_call_target="InvertDiagBlocksLowerTriangular" | custom-call | tf_op jit(solution)/shard_map/triangular_solve | solution.py:64
  145.3 3.0 convolution_bitcast_fusion
  148.3 2.0 fusion.22
  150.4 12.5 %while.33 = (s32[]{:T(128)}, f32[8,128,128]{2,1,0:T(8,128)S(1)}, f32[8,128,128]{2,1,0:T(8,128)}, f32[2,8,128,128]{3,2,0,1:T(8,128)}, f32[2,8,128,128]{2,3,0,1:T(...) while((s32[]{:T(128)}, f32[8,128,128]{2,1,0:T(8,128)S(1)}, ...), condition=%wide.region_7.8_spmd.clone, body=%wide.region_6.7_spmd.clone.sunk | while | flops 403046400 | bytes 9963628 | solution.py:120
  151.5 2.5 convolution_add_fusion.5
  157.7 2.5 convolution_add_fusion.5
  164.9 2.8 convolution_multiply_fusion
  167.8 104.3 %all-gather.6.cloned.1.call-done = f32[128,128,128]{2,1,0:T(8,128)} async-done(((f32[8,128,128]{2,1,0:T(8,128)}), f32[128,128,128]{2,1,0:T(8,128)}) %all-gather.6.cloned.1.call-update) | async-done | bytes 8388624 | tf_op jit(solution)/shard_map/all_gather | solution.py:12
  272.0 113.3 %all-gather.8.cloned.1.call-done = f32[128,128,128]{2,1,0:T(8,128)} async-done(((f32[8,128,128]{2,1,0:T(8,128)}), f32[128,128,128]{2,1,0:T(8,128)}) %all-gather.8.cloned.1.call-update) | async-done | bytes 8388624 | tf_op jit(solution)/shard_map/all_gather | solution.py:12
  385.4 55.4 %while.34 = (s32[]{:T(128)}, f32[8,128,128]{2,1,0:T(8,128)S(1)}, f32[8,128,128]{2,1,0:T(8,128)S(1)}, s32[]{:T(128)}, f32[16,8,128,128]{3,2,1,0:T(8,128)}, /*index=5*/f32[16,8,128,128]{3,2,1,0:T(8,128)}, s32[]{:T(128)}, s32[]{:T(128)}) while((s32[]{:T(128)}, f32[8,128,128]{2,1,0:T(8,128)S(1)}, f32[8,128,128]{2,1,0:T(8,128)S(1)}, ...), condition=%wide.region_9.10_spmd.clone, body=%wide.region_8.9_spmd.clone.sunk | while | flops 403308544 | bytes 6818920 | solution.py:21
  385.4 1.9 fusion.102
  387.4 1.7 convolution_select_fusion.2
  389.2 1.9 fusion.102
  391.1 1.7 convolution_select_fusion.2
  392.9 1.9 fusion.102
  394.8 1.7 convolution_select_fusion.2
  396.6 1.9 fusion.102
  398.5 1.7 convolution_select_fusion.2
  400.3 1.9 fusion.102
  402.2 1.7 convolution_select_fusion.2
  403.9 1.9 fusion.102
  405.9 1.7 convolution_select_fusion.2
  407.6 1.9 fusion.102
  409.6 1.7 convolution_select_fusion.2
  411.3 1.9 fusion.102
  413.2 1.7 convolution_select_fusion.2
  415.0 1.9 fusion.102
  416.9 1.7 convolution_select_fusion.2
  418.7 1.9 fusion.102
  420.6 1.7 convolution_select_fusion.2
  422.4 1.9 fusion.102
  424.3 1.7 convolution_select_fusion.2
  426.1 1.9 fusion.102
  428.0 1.7 convolution_select_fusion.2
  429.8 1.9 fusion.102
  431.7 1.7 convolution_select_fusion.2
  433.5 1.9 fusion.102
  435.4 1.7 convolution_select_fusion.2
  437.1 1.9 fusion.102
  439.1 1.7 convolution_select_fusion.2
  441.5 2.6 fusion.23
  444.1 2.9 convolution_subtract_fusion
  447.0 1.3 copy.94
  448.3 1.8 fusion.69
  450.1 2.2 fusion.45
  (108 shorter events, 23.1 us)
Async XLA Ops:
  7.2 433.6 %copy-start = (f32[8,128,128]{2,1,0:T(8,128)S(1)}, f32[8,128,128]{2,1,0:T(8,128)}, u32[]{:S(2)}) copy-start(f32[8,128,128]{2,1,0:T(8,128)} %param.19) | copy-start | bytes 1572868
  7.2 264.9 %all-gather.6.cloned.1.call-start = ((), (), s32[]{:S(2)}) async-start(), calls=%async_computation | async-start | bytes 8912896 | tf_op jit(solution)/shard_map/all_gather | solution.py:12
  57.2 91.0 %copy-start.2 = (f32[128,8,128]{2,0,1:T(8,128)}, f32[128,8,128]{2,0,1:T(8,128)S(1)}, u32[]{:S(2)}) copy-start(f32[128,8,128]{2,0,1:T(8,128)S(1)} %copy.77) | copy-start | bytes 1572868
  145.3 5.0 %copy-start.3 = (f32[8,2,64,256]{3,2,1,0:T(8,128)}, f32[8,2,64,256]{3,2,1,0:T(8,128)S(1)}, u32[]{:S(2)}) copy-start(f32[8,2,64,256]{3,2,1,0:T(8,128)S(1)} %fusion.31) | copy-start | bytes 3145732
  150.3 14.1 %copy-start.5 = (bf16[128,8,128]{2,1,0:T(8,128)(2,1)S(1)}, bf16[128,8,128]{2,1,0:T(8,128)(2,1)}, u32[]{:S(2)}) copy-start(bf16[128,8,128]{2,1,0:T(8,128)(2,1)} %param.12) | copy-start | bytes 786436
  162.8 0.8 copy-start.1
  163.7 221.7 %all-gather.8.cloned.1.call-start = ((), (), s32[]{:S(2)}) async-start(), calls=%async_computation.1 | async-start | bytes 8912896 | tf_op jit(solution)/shard_map/all_gather | solution.py:12
  385.4 58.7 %copy-start.4 = (f32[8,2,64,256]{3,2,1,0:T(8,128)S(1)}, f32[8,2,64,256]{3,2,1,0:T(8,128)}, u32[]{:S(2)}) copy-start(f32[8,2,64,256]{3,2,1,0:T(8,128)} %copy-done.3) | copy-start | bytes 3145732
  440.8 11.7 %copy-start.6 = (bf16[128,8,128]{2,1,0:T(8,128)(2,1)S(1)}, bf16[128,8,128]{2,1,0:T(8,128)(2,1)}, u32[]{:S(2)}) copy-start(bf16[128,8,128]{2,1,0:T(8,128)(2,1)} %param.15) | copy-start | bytes 786436
Sparse Core Ops, SparseCore 0:
  163.8 108.2 all-gather.5
  274.8 110.4 all-gather.7
